TPU v7x, 256 devices: a whole 4x4x8 slice. The times are simulated.
256 devices in a mesh: seq: 64 (over x_hi, y, z), head: 4 (over x_lo, core).
Axes of the slice: x: 4 (x_hi: 2, x_lo: 2; x = x_hi * 2 + x_lo), y: 4, z: 8, core: 2. Of those that a mesh axis runs over, the one named last changes fastest.
Arguments:
- queries: bfloat16 [98304, 2048], P('seq', 'head'), may hold values from -200 to 200
- keys_values: bfloat16 [2, 98304, 2048], P(None, 'seq', 'head'), may hold values from -6 to 6
- global_ids: int32 [2], replicated, may hold values from 0 to 1535
- rand_ids: int32 [1536, 3], replicated, may hold values from 0 to 1535, as said below
- out_weight: bfloat16 [2048, 4096], P(None, 'head'), may hold values from -2 to 2
Outputs:
- projected: bfloat16 [98304, 4096], P('seq', 'head')
Inputs may be any that keep to these rules, and one draw needn't show every extreme that they name: `rand_ids`: row i lists the 3 random key blocks of query block i. Among the 24 rows of one seq shard, at most 2 listed blocks lie on any one shard, and at most 1 of one column do; both bounds are reached.
All inputs are finite; a program needn't handle non-finite values.
Results may differ from a plain program's by a relative error of at most 0.0057.
Values may be sent and summed in bfloat16 or wider, within the bound.
A program may use at most 128 MiB of HBM per device.

v0:
```python
import jax
import jax.numpy as jnp
from jax import lax
from jax.sharding import PartitionSpec as P

HEAD_DIM = 128
BLOCK = 64
NGLOBAL = 2
NRANDOM = 3
group_blocks = 8


def padded_2(block, sides, width):
    for axis, dim in sides:
        count = lax.axis_size(axis)
        forward = [(i, i + 1) for i in range(count - 1)]
        backward = [(target, source) for source, target in forward]
        low = lax.ppermute(
            lax.slice_in_dim(block, block.shape[dim] - width, None, axis=dim), axis, forward
        )
        high = lax.ppermute(lax.slice_in_dim(block, 0, width, axis=dim), axis, backward)
        block = jnp.concatenate([low, block, high], axis=dim)
    return block


def broadcast(block, axis, owner):
    block = jnp.where(lax.axis_index(axis) == owner, block, jnp.zeros_like(block))
    return lax.psum(block, axis)


def plan_slots(requests, myself, capacity, per_shard):
    sources = requests // per_shard
    offsets = requests % per_shard
    count = requests.shape[1]
    order = jnp.arange(count, dtype=jnp.int32)
    earlier = (order[:, None] < order[None, :]).astype(jnp.int32)
    matches = (sources[:, :, None] == sources[:, None, :]).astype(jnp.int32)
    ranks = jnp.sum(matches * earlier[None], axis=1)
    slot_range = jnp.arange(capacity, dtype=jnp.int32)
    wanted = (
        (sources == myself)[:, None, :] & (ranks[:, None, :] == slot_range[None, :, None])
    ).astype(jnp.int32)
    chosen = jnp.sum(wanted * offsets[:, None, :], axis=2).reshape(-1)
    own_sources = lax.dynamic_index_in_dim(sources, myself, 0, keepdims=False)
    own_ranks = lax.dynamic_index_in_dim(ranks, myself, 0, keepdims=False)
    return (chosen, own_sources * capacity + own_ranks)


def attend_blocks(query_part, local_keys, local_values, glob_keys, glob_values, valid):
    scale = 1.0 / HEAD_DIM**0.5
    near_scores = (
        jnp.einsum("bqhd,bkhd->bhqk", query_part, local_keys, preferred_element_type=jnp.float32)
        * scale
    )
    near_scores = jnp.where(valid[:, None, None, :], near_scores, -jnp.inf)
    glob_scores = (
        jnp.einsum("bqhd,khd->bhqk", query_part, glob_keys, preferred_element_type=jnp.float32)
        * scale
    )
    highest = jnp.maximum(jnp.max(near_scores, axis=-1), jnp.max(glob_scores, axis=-1))
    near_exp = jnp.exp(near_scores - highest[..., None])
    glob_exp = jnp.exp(glob_scores - highest[..., None])
    total = jnp.sum(near_exp, axis=-1) + jnp.sum(glob_exp, axis=-1)
    near_weights = (near_exp / total[..., None]).astype(jnp.bfloat16)
    glob_weights = (glob_exp / total[..., None]).astype(jnp.bfloat16)
    mixed = jnp.einsum(
        "bhqk,bkhd->bqhd", near_weights, local_values, preferred_element_type=jnp.float32
    )
    mixed = mixed + jnp.einsum(
        "bhqk,khd->bqhd", glob_weights, glob_values, preferred_element_type=jnp.float32
    )
    return mixed.astype(jnp.bfloat16)


def body(queries, keys_values, global_ids, rand_ids, out_weight):
    rows = queries.shape[0]
    width = queries.shape[1]
    heads_here = width // HEAD_DIM
    local_blocks = rows // BLOCK
    shards = lax.axis_size("seq")
    myself = lax.axis_index("seq")
    total_blocks = local_blocks * shards
    pair_blocks = keys_values.reshape(2, local_blocks, BLOCK, width)
    padded = padded_2(keys_values, (("seq", 1),), BLOCK)
    padded = padded.reshape(2, local_blocks + 2, BLOCK, width)
    panel_list = []
    for which in range(NGLOBAL):
        target = global_ids[which]
        owner = target // local_blocks
        local_panel = lax.dynamic_index_in_dim(
            pair_blocks, target % local_blocks, 1, keepdims=False
        )
        panel_list.append(broadcast(local_panel, "seq", owner))
    glob = jnp.stack(panel_list, axis=1).reshape(2, NGLOBAL * BLOCK, heads_here, HEAD_DIM)
    requests = rand_ids.reshape(shards, local_blocks, NRANDOM)
    capacity = (local_blocks + shards - 1) // shards
    fetched = []
    for column in range(NRANDOM):
        chosen, slots = plan_slots(requests[:, :, column], myself, capacity, local_blocks)
        outgoing = jnp.take(pair_blocks, chosen, axis=1)
        incoming = lax.all_to_all(outgoing, "seq", split_axis=1, concat_axis=1, tiled=True)
        fetched.append(jnp.take(incoming, slots, axis=1))
    remote = jnp.stack(fetched, axis=2)
    segment = jnp.arange((3 + NRANDOM) * BLOCK, dtype=jnp.int32) // BLOCK

    def one_group(index):
        first = index * group_blocks
        query_part = lax.dynamic_slice_in_dim(queries, first * BLOCK, group_blocks * BLOCK, 0)
        query_part = query_part.reshape(group_blocks, BLOCK, heads_here, HEAD_DIM)
        window = lax.dynamic_slice_in_dim(padded, first, group_blocks + 2, 1)
        farther = lax.dynamic_slice_in_dim(remote, first, group_blocks, 1)
        farther = farther.reshape(2, group_blocks, NRANDOM * BLOCK, width)
        local = jnp.concatenate(
            [
                window[:, 0:group_blocks],
                window[:, 1 : group_blocks + 1],
                window[:, 2 : group_blocks + 2],
                farther,
            ],
            axis=2,
        )
        local = local.reshape(2, group_blocks, (3 + NRANDOM) * BLOCK, heads_here, HEAD_DIM)
        block_ids = myself * local_blocks + first + jnp.arange(group_blocks, dtype=jnp.int32)
        drop_before = (segment[None, :] == 0) & (block_ids[:, None] == 0)
        drop_after = (segment[None, :] == 2) & (block_ids[:, None] == total_blocks - 1)
        valid = jnp.logical_not(drop_before | drop_after)
        mixed = attend_blocks(query_part, local[0], local[1], glob[0], glob[1], valid)
        return mixed.reshape(group_blocks * BLOCK, width)

    attended = lax.map(
        one_group, jnp.arange(local_blocks // group_blocks, dtype=jnp.int32)
    ).reshape(rows, width)
    summed = jnp.dot(
        lax.all_gather(attended, "head", axis=1, tiled=True),
        out_weight,
        preferred_element_type=jnp.float32,
    )
    return summed.astype(jnp.bfloat16)


def solution(mesh):
    in_specs = (P("seq", "head"), P(None, "seq", "head"), P(), P(), P(None, "head"))
    out_specs = P("seq", "head")
    return jax.shard_map(body, mesh=mesh, in_specs=in_specs, out_specs=out_specs, check_vma=False)
```

profile of v0, /device:TPU:1, one launch (start us, length us, event | category | flops | bytes accessed | tf_op | source)
XLA Modules:
  0.0 1352.4 jit_solution(5042256346633394672)
XLA Ops:
  8.1 7.2 gather_fusion.2
  15.3 7.5 select_bitcast_fusion.1
  22.8 15.6 %all-to-all-start.1 = ((bf16[2,64,64,512]{3,2,0,1:T(8,128)(2,1)}), bf16[2,64,64,512]{3,2,0,1:T(8,128)(2,1)}, u32[]{:S(2)}, u32[]{:S(2)}) async-start(bf16[2,64,64,512]{3,2,0,1:T(8,128)(2,1)} %select_bitcast_fusion.1), calls=%async_computation.1 | async-start | bytes 16777216 | tf_op jit(solution)/shard_map/all_to_all | solution.py:101
  38.6 5.5 gather_fusion
  44.1 7.5 select_bitcast_fusion.2
  51.5 169.7 %all-to-all-done.1 = bf16[2,64,64,512]{3,2,0,1:T(8,128)(2,1)} async-done(((bf16[2,64,64,512]{3,2,0,1:T(8,128)(2,1)}), bf16[2,64,64,512]{3,2,0,1:T(8,128)(2,1)}, u32[]{:S(2)}, u32[]{:S(2)}) %all-to-all-start.1) | async-done | bytes 8388640 | tf_op jit(solution)/shard_map/all_to_all | solution.py:101
  221.2 12.9 all-to-all-start
  234.1 5.2 gather_fusion.4
  239.3 7.5 select_bitcast_fusion
  246.8 169.9 %all-to-all-done = bf16[2,64,64,512]{3,2,0,1:T(8,128)(2,1)} async-done(((bf16[2,64,64,512]{3,2,0,1:T(8,128)(2,1)}), bf16[2,64,64,512]{3,2,0,1:T(8,128)(2,1)}, u32[]{:S(2)}, u32[]{:S(2)}) %all-to-all-start) | async-done | bytes 8388640 | tf_op jit(solution)/shard_map/all_to_all | solution.py:101
  416.7 13.1 all-to-all-start.2
  429.9 2.8 collective-permute-start
  444.4 169.5 %collective-permute-done = bf16[2,64,512]{2,1,0:T(8,128)(2,1)S(1)} collective-permute-done((bf16[2,64,512]{2,1,0:T(8,128)(2,1)S(1)}, bf16[2,64,512]{2,1,0:T(8,128)(2,1)S(1)}, u32[]{:S(2)}, u32[]{:S(2)}) %collective-permute-start) | collective-permute-done | bytes 131104 | tf_op jit(solution)/shard_map/ppermute | solution.py:18
  615.6 2.7 pad_maximum_fusion.2
  618.3 454.0 %all-reduce.3.cloned.1.call-done = (bf16[2,1,64,512]{3,2,1,0:T(8,128)(2,1)}, bf16[2,1,64,512]{3,2,1,0:T(8,128)(2,1)}) async-done(((bf16[2,1,64,512]{3,2,1,0:T(8,128)(2,1)}, bf16[2,1,64,512]{3,2,1,0:T(8,128)(2,1)}), (bf16[2,1,64,512]{3,2,1,0:T(8,128)(2,1)}, bf16[2,1,64,512]{3,2,1,0:T(8,128)(2,1)})) %all-reduce.3.cloned.1.call-update) | async-done | bytes 262160 | tf_op jit(solution)/shard_map/psum | solution.py:28
  1073.4 7.7 copy.122
  1081.1 5.9 gather_fusion.3
  1087.0 7.7 copy.120
  1094.7 5.9 gather_fusion.1
  1100.6 2.4 select_bitcast_fusion.4
  1105.5 7.7 copy.124
  1113.2 5.9 gather_fusion.5
  1119.1 2.4 select_bitcast_fusion.3
  1121.9 4.2 pad_maximum_fusion.1
  1126.1 114.5 %while.14 = (s32[]{:T(128)}, bf16[3,512,512]{2,1,0:T(8,128)(2,1)}, s32[3]{0:T(128)S(1)}, bf16[2,26,64,512]{3,2,1,0:T(8,128)(2,1)}, bf16[2,24,3,64,512]{4,3,0,1,2...) while((s32[]{:T(128)}, bf16[3,512,512]{2,1,0:T(8,128)(2,1)}, ...), condition=%wide.region_13.16_spmd.clone.clone, body=%wide.region_8.15_spmd.clone.clone.sunk | while | flops 573845248 | bytes 120519192 | solution.py:130
  1127.2 2.3 constant_dynamic-slice_fusion.9
  1129.6 2.2 constant_dynamic-slice_fusion.8
  1132.2 4.8 pad_maximum_fusion.5
  1137.0 3.3 fusion.73
  1140.3 3.4 copy.164
  1153.8 4.8 copy.163
  1158.5 3.3 fusion.80
  1165.5 2.4 constant_dynamic-slice_fusion.9
  1167.8 2.2 constant_dynamic-slice_fusion.8
  1170.4 4.8 pad_maximum_fusion.5
  1175.2 3.3 fusion.73
  1178.6 3.4 copy.164
  1192.0 4.8 copy.163
  1196.8 3.3 fusion.80
  1203.7 2.1 constant_dynamic-slice_fusion.9
  1205.9 2.2 constant_dynamic-slice_fusion.8
  1208.5 4.8 pad_maximum_fusion.5
  1213.3 3.3 fusion.73
  1216.6 3.4 copy.164
  1230.0 4.8 copy.163
  1234.8 3.3 fusion.80
  1240.6 93.8 %all-gather.2.cloned.1.call-done = bf16[1536,2048]{1,0:T(8,128)(2,1)} async-done(((bf16[1536,512]{1,0:T(8,128)(2,1)}), bf16[1536,2048]{1,0:T(8,128)(2,1)}) %all-gather.2.cloned.1.call-update) | async-done | bytes 6291472 | tf_op jit(solution)/shard_map/all_gather | solution.py:134
  1334.4 11.1 convolution_convert_fusion
  (159 shorter events, 53.1 us)
Async XLA Ops:
  7.6 7.7 copy-start.8
  7.7 7.6 copy-start.9
  8.0 7.4 copy-start.11
  8.0 7.4 copy-start.12
  8.0 30.5 %copy-start.10 = (s32[64,24]{0,1:T(8,128)}, s32[64,24]{0,1:T(8,128)S(1)}, u32[]{:S(2)}) copy-start(s32[64,24]{0,1:T(8,128)S(1)} %get-tuple-element.222) | copy-start | bytes 18436
  22.8 15.7 %copy-start.2 = (bf16[2,1536,512]{2,1,0:T(8,128)(2,1)S(1)}, bf16[2,1536,512]{2,1,0:T(8,128)(2,1)}, u32[]{:S(2)}) copy-start(bf16[2,1536,512]{2,1,0:T(8,128)(2,1)} %param.12) | copy-start | bytes 9437188
  22.8 198.4 %all-to-all-start.1 = ((bf16[2,64,64,512]{3,2,0,1:T(8,128)(2,1)}), bf16[2,64,64,512]{3,2,0,1:T(8,128)(2,1)}, u32[]{:S(2)}, u32[]{:S(2)}) async-start(bf16[2,64,64,512]{3,2,0,1:T(8,128)(2,1)} %select_bitcast_fusion.1), calls=%async_computation.1 | async-start | bytes 16777216 | tf_op jit(solution)/shard_map/all_to_all | solution.py:101
  221.2 195.5 %all-to-all-start = ((bf16[2,64,64,512]{3,2,0,1:T(8,128)(2,1)}), bf16[2,64,64,512]{3,2,0,1:T(8,128)(2,1)}, u32[]{:S(2)}, u32[]{:S(2)}) async-start(bf16[2,64,64,512]{3,2,0,1:T(8,128)(2,1)} %select_bitcast_fusion.2), calls=%async_computation | async-start | bytes 16777216 | tf_op jit(solution)/shard_map/all_to_all | solution.py:101
  246.8 187.3 %copy-start.14 = (s32[2]{0:T(128)S(1)}, s32[2]{0:T(128)}, u32[]{:S(2)}) copy-start(s32[2]{0:T(128)} %param.13) | copy-start | bytes 28
  416.7 688.8 %all-to-all-start.2 = ((bf16[2,64,64,512]{3,2,0,1:T(8,128)(2,1)}), bf16[2,64,64,512]{3,2,0,1:T(8,128)(2,1)}, u32[]{:S(2)}, u32[]{:S(2)}) async-start(bf16[2,64,64,512]{3,2,0,1:T(8,128)(2,1)} %select_bitcast_fusion), calls=%async_computation.2 | async-start | bytes 16777216 | tf_op jit(solution)/shard_map/all_to_all | solution.py:101
  429.8 642.5 %all-reduce.3.cloned.1.call-start = ((), (), s32[]{:S(2)}) async-start(), calls=%async_computation.4 | async-start | bytes 524288 | tf_op jit(solution)/shard_map/psum | solution.py:28
  429.9 184.1 %collective-permute-start = (bf16[2,64,512]{2,1,0:T(8,128)(2,1)S(1)}, bf16[2,64,512]{2,1,0:T(8,128)(2,1)S(1)}, u32[]{:S(2)}, u32[]{:S(2)}) collective-permute-start(bf16[2,64,512]{2,1,0:T(8,128)(2,1)S(1)} %get-tuple-element.258), channel_id=1, source_target_pairs={{0,4},{4,8},{8,12},{12,16},{16,20},{20,24},{24,28},{28,32},{32,36}... | collective-permute-start | bytes 393224 | tf_op jit(solution)/shard_map/ppermute | solution.py:18
  432.7 182.9 %collective-permute-start.1 = (bf16[2,64,512]{2,1,0:T(8,128)(2,1)S(1)}, bf16[2,64,512]{2,1,0:T(8,128)(2,1)}, u32[]{:S(2)}, u32[]{:S(2)}) collective-permute-start(bf16[2,64,512]{2,1,0:T(8,128)(2,1)S(1)} %get-tuple-element.259), channel_id=1, source_target_pairs={{4,0},{8,4},{12,8},{16,12},{20,16},{24,20},{28,24},{32,28},{36,32}... | collective-permute-start | bytes 393224 | tf_op jit(solution)/shard_map/ppermute | solution.py:21
  439.1 895.4 %all-gather.2.cloned.1.call-start = ((), (), s32[]{:S(2)}) async-start(), calls=%async_computation.3 | async-start | bytes 7864320 | tf_op jit(solution)/shard_map/all_gather | solution.py:134
  1094.7 5.9 copy-start.13
  1100.6 2.8 copy-start.7
  1100.6 2.8 copy-start.15
  1119.1 2.8 copy-start.6
  1148.3 2.0 copy-start.3
  1150.2 1.6 copy-start
  1150.8 3.0 copy-start.4
  1153.7 4.8 copy-start.1
  1158.5 3.4 copy-start.5
  1186.5 2.0 copy-start.3
  1188.5 1.6 copy-start
  1189.0 3.0 copy-start.4
  1192.0 4.8 copy-start.1
  1196.8 3.4 copy-start.5
  1224.5 2.0 copy-start.3
  1226.5 1.6 copy-start
  1227.0 3.0 copy-start.4
  1230.0 4.8 copy-start.1
  1234.8 3.4 copy-start.5
Sparse Core Ops, SparseCore 0:
  439.2 633.0 all-reduce.2
  1240.8 93.6 all-gather.1
where the time goes:
time: 1350 us
  waiting for transfers between devices  1060 us (79%)
  local copies, waits for them, and re-layouts  131 us (10%)
  other arithmetic  63.6 us (5%)
  starting transfers between devices  46.1 us (3%)
  matrix products  31.4 us (2%)
  between operations  17.4 us (1%)
    psum x1, waiting for transfers between devices, broadcast(): return lax.psum(block, axis)  454 us
    all_to_all x3, waiting for transfers between devices, body(): lax.all_to_all(outgoing, 'seq', split_axis=1, concat_axis=1, tiled=True)  340 us
    ppermute x1, waiting for transfers between devices, padded_2(): lax.ppermute(lax.slice_in_dim(block, block.shape[dim] - width, None, axis...  170 us
    all_gather x1, waiting for transfers between devices, body(): lax.all_gather(attended, 'head', axis=1, tiled=True)  93.8 us
    all_to_all x3, starting transfers between devices, body(): lax.all_to_all(outgoing, 'seq', split_axis=1, concat_axis=1, tiled=True)  41.7 us
  transfers between devices with their start and end apart: 7, of which 6 were waited for; matrix products, arithmetic and copies ran while one was open for 5% of the time, Pallas kernels for 0%

commit v1 on v0

--- a/solution.py
+++ b/solution.py
@@ -2,12 +2,17 @@
 import jax.numpy as jnp
 from jax import lax
 from jax.sharding import PartitionSpec as P
+from jax.lax import all_gather
 
 HEAD_DIM = 128
 BLOCK = 64
 NGLOBAL = 2
 NRANDOM = 3
 group_blocks = 8
+
+
+def number_sources_all(tile_in, mesh_dim):
+    return jnp.sum(all_gather(tile_in, mesh_dim), axis=0)
 
 
 def padded_2(block, sides, width):
@@ -25,7 +30,7 @@
 
 def broadcast(block, axis, owner):
     block = jnp.where(lax.axis_index(axis) == owner, block, jnp.zeros_like(block))
-    return lax.psum(block, axis)
+    return number_sources_all(block, axis)
 
 
 def plan_slots(requests, myself, capacity, per_shard):

time: 1350 us -> 948 us (0.70)
  waiting for transfers between devices: 1060 us -> 632 us
    psum x1 -> x0, waiting for transfers between devices: 454 us -> none  [broadcast(): return lax.psum(block, axis)]
    all_to_all x3, waiting for transfers between devices: 340 us -> 388 us  [body(): lax.all_to_all(outgoing, 'seq', split_axis=1, concat_axis=1, tiled=True)]
    all_gather x1, waiting for transfers between devices: 93.8 us -> 74.9 us  [body(): lax.all_gather(attended, 'head', axis=1, tiled=True)]
  transfers between devices with their start and end apart: 7 -> 8, of which waited for: 6 -> 5; matrix products, arithmetic and copies ran while one was open for 5% -> 8% of each run, Pallas kernels for 0% -> 0%
where the time goes in v1:
time: 948 us; the launch traced here: 946 us
  waiting for transfers between devices  632 us (67%)
  local copies, waits for them, and re-layouts  132 us (14%)
  other arithmetic  71.7 us (8%)
  starting transfers between devices  57.4 us (6%)
  matrix products  31.4 us (3%)
  between operations  17.5 us (2%)
    all_to_all x3, waiting for transfers between devices, body(): lax.all_to_all(outgoing, 'seq', split_axis=1, concat_axis=1, tiled=True)  388 us
    ppermute x1, waiting for transfers between devices, padded_2(): lax.ppermute(lax.slice_in_dim(block, block.shape[dim] - width, None, axis...  162 us
    all_gather x1, waiting for transfers between devices, body(): lax.all_gather(attended, 'head', axis=1, tiled=True)  74.9 us
    all_to_all x3, starting transfers between devices, body(): lax.all_to_all(outgoing, 'seq', split_axis=1, concat_axis=1, tiled=True)  53 us
    all_to_all x3, local copies, waits for them, and re-layouts, body(): lax.all_to_all(outgoing, 'seq', split_axis=1, concat_axis=1, tiled=True)  23.3 us
    select_n x5, other arithmetic, body(): outgoing = jnp.take(pair_blocks, chosen, axis=1)  22.5 us
    slice x6, local copies, waits for them, and re-layouts, one_group(): local[0]  20.2 us
  transfers between devices with their start and end apart: 8, of which 5 were waited for; matrix products, arithmetic and copies ran while one was open for 8% of the time, Pallas kernels for 0%

profile of v1, /device:TPU:1, one launch (start us, length us, event | category | flops | bytes accessed | tf_op | source)
XLA Modules:
  0.0 946.4 jit_solution(8225001316482457517)
XLA Ops:
  8.1 7.2 gather_fusion.2
  15.3 7.5 select_bitcast_fusion.1
  22.8 15.6 %all-to-all-start.1 = ((bf16[2,64,64,512]{3,2,0,1:T(8,128)(2,1)}), bf16[2,64,64,512]{3,2,0,1:T(8,128)(2,1)}, u32[]{:S(2)}, u32[]{:S(2)}) async-start(bf16[2,64,64,512]{3,2,0,1:T(8,128)(2,1)} %select_bitcast_fusion.1), calls=%async_computation.1 | async-start | bytes 16777216 | tf_op jit(solution)/shard_map/all_to_all | solution.py:106
  44.1 5.6 gather_fusion
  49.7 7.6 select_bitcast_fusion.2
  57.2 191.7 %all-to-all-done.1 = bf16[2,64,64,512]{3,2,0,1:T(8,128)(2,1)} async-done(((bf16[2,64,64,512]{3,2,0,1:T(8,128)(2,1)}), bf16[2,64,64,512]{3,2,0,1:T(8,128)(2,1)}, u32[]{:S(2)}, u32[]{:S(2)}) %all-to-all-start.1) | async-done | bytes 8388640 | tf_op jit(solution)/shard_map/all_to_all | solution.py:106
  249.0 19.2 %all-to-all-start = ((bf16[2,64,64,512]{3,2,0,1:T(8,128)(2,1)}), bf16[2,64,64,512]{3,2,0,1:T(8,128)(2,1)}, u32[]{:S(2)}, u32[]{:S(2)}) async-start(bf16[2,64,64,512]{3,2,0,1:T(8,128)(2,1)} %select_bitcast_fusion.2), calls=%async_computation | async-start | bytes 16777216 | tf_op jit(solution)/shard_map/all_to_all | solution.py:106
  269.0 5.2 gather_fusion.4
  274.2 7.5 select_bitcast_fusion
  281.7 196.4 %all-to-all-done = bf16[2,64,64,512]{3,2,0,1:T(8,128)(2,1)} async-done(((bf16[2,64,64,512]{3,2,0,1:T(8,128)(2,1)}), bf16[2,64,64,512]{3,2,0,1:T(8,128)(2,1)}, u32[]{:S(2)}, u32[]{:S(2)}) %all-to-all-start) | async-done | bytes 8388640 | tf_op jit(solution)/shard_map/all_to_all | solution.py:106
  478.1 18.1 %all-to-all-start.2 = ((bf16[2,64,64,512]{3,2,0,1:T(8,128)(2,1)}), bf16[2,64,64,512]{3,2,0,1:T(8,128)(2,1)}, u32[]{:S(2)}, u32[]{:S(2)}) async-start(bf16[2,64,64,512]{3,2,0,1:T(8,128)(2,1)} %select_bitcast_fusion), calls=%async_computation.2 | async-start | bytes 16777216 | tf_op jit(solution)/shard_map/all_to_all | solution.py:106
  496.2 2.8 collective-permute-start
  505.6 162.2 %collective-permute-done = bf16[2,64,512]{2,1,0:T(8,128)(2,1)S(1)} collective-permute-done((bf16[2,64,512]{2,1,0:T(8,128)(2,1)S(1)}, bf16[2,64,512]{2,1,0:T(8,128)(2,1)S(1)}, u32[]{:S(2)}, u32[]{:S(2)}) %collective-permute-start) | collective-permute-done | bytes 131104 | tf_op jit(solution)/shard_map/ppermute | solution.py:23
  667.8 6.1 collective-permute-done.1
  673.9 2.7 pad_maximum_fusion.2
  676.6 4.6 bitcast_reduce_fusion.1
  681.2 4.6 bitcast_reduce_fusion
  686.0 7.8 copy.122
  693.7 5.9 gather_fusion.3
  699.6 7.8 copy.120
  707.4 5.8 gather_fusion.1
  713.3 2.4 select_bitcast_fusion.4
  718.1 7.7 copy.124
  725.8 5.9 gather_fusion.5
  731.7 2.4 select_bitcast_fusion.3
  734.6 4.1 pad_maximum_fusion.1
  738.6 115.1 %while.14 = (s32[]{:T(128)}, bf16[3,512,512]{2,1,0:T(8,128)(2,1)}, s32[3]{0:T(128)S(1)}, bf16[2,26,64,512]{3,2,1,0:T(8,128)(2,1)}, bf16[2,24,3,64,512]{4,3,0,1,2...) while((s32[]{:T(128)}, bf16[3,512,512]{2,1,0:T(8,128)(2,1)}, ...), condition=%wide.region_13.16_spmd.clone.clone, body=%wide.region_8.15_spmd.clone.clone.sunk | while | flops 573845248 | bytes 120519192 | solution.py:135
  742.1 2.2 constant_dynamic-slice_fusion.8
  744.7 4.8 pad_maximum_fusion.5
  749.5 3.3 fusion.73
  752.8 3.4 copy.164
  766.3 4.8 copy.163
  771.1 3.3 fusion.80
  778.3 2.3 constant_dynamic-slice_fusion.9
  780.6 2.2 constant_dynamic-slice_fusion.8
  783.2 4.8 pad_maximum_fusion.5
  788.0 3.3 fusion.73
  791.3 3.4 copy.164
  804.8 4.8 copy.163
  809.6 3.3 fusion.80
  818.9 2.2 constant_dynamic-slice_fusion.8
  821.5 4.8 pad_maximum_fusion.5
  826.3 3.3 fusion.73
  829.6 3.4 copy.164
  843.2 4.8 copy.163
  848.0 3.3 fusion.80
  853.8 74.9 %all-gather.6.cloned.1.call-done = bf16[1536,2048]{1,0:T(8,128)(2,1)} async-done(((bf16[1536,512]{1,0:T(8,128)(2,1)}), bf16[1536,2048]{1,0:T(8,128)(2,1)}) %all-gather.6.cloned.1.call-update) | async-done | bytes 6291472 | tf_op jit(solution)/shard_map/all_gather | solution.py:139
  928.7 11.1 %convolution_convert_fusion = bf16[1536,1024]{1,0:T(8,128)(2,1)} fusion(bf16[1536,2048]{1,0:T(8,128)(2,1)} %all-gather.6.cloned.1.call-done, bf16[2048,1024]{1,0:T(8,128)(2,1)} %param.15), kind=kOutput, calls=%fused_computation.61 | convolution fusion | flops 6444023808 | bytes 13631488 | tf_op jit(solution)/shard_map/dot_general | solution.py:138
  (164 shorter events, 55.7 us)
Async XLA Ops:
  7.6 7.7 copy-start.8
  7.7 7.6 copy-start.9
  8.0 7.4 copy-start.11
  8.0 7.3 copy-start.12
  8.0 36.0 %copy-start.10 = (s32[64,24]{0,1:T(8,128)}, s32[64,24]{0,1:T(8,128)S(1)}, u32[]{:S(2)}) copy-start(s32[64,24]{0,1:T(8,128)S(1)} %get-tuple-element.222) | copy-start | bytes 18436
  22.8 15.7 %copy-start.14 = (s32[2]{0:T(128)S(1)}, s32[2]{0:T(128)}, u32[]{:S(2)}) copy-start(s32[2]{0:T(128)} %param.13) | copy-start | bytes 28
  22.8 20.4 %copy-start.2 = (bf16[2,1536,512]{2,1,0:T(8,128)(2,1)S(1)}, bf16[2,1536,512]{2,1,0:T(8,128)(2,1)}, u32[]{:S(2)}) copy-start(bf16[2,1536,512]{2,1,0:T(8,128)(2,1)} %param.12) | copy-start | bytes 9437188
  22.8 226.2 %all-to-all-start.1 = ((bf16[2,64,64,512]{3,2,0,1:T(8,128)(2,1)}), bf16[2,64,64,512]{3,2,0,1:T(8,128)(2,1)}, u32[]{:S(2)}, u32[]{:S(2)}) async-start(bf16[2,64,64,512]{3,2,0,1:T(8,128)(2,1)} %select_bitcast_fusion.1), calls=%async_computation.1 | async-start | bytes 16777216 | tf_op jit(solution)/shard_map/all_to_all | solution.py:106
  38.5 638.1 %all-gather.8.cloned.1.call-start = ((), (), s32[]{:S(2)}) async-start(), calls=%async_computation.4 | async-start | bytes 8519680 | tf_op jit(solution)/shard_map/all_gather | solution.py:15
  249.0 229.1 %all-to-all-start = ((bf16[2,64,64,512]{3,2,0,1:T(8,128)(2,1)}), bf16[2,64,64,512]{3,2,0,1:T(8,128)(2,1)}, u32[]{:S(2)}, u32[]{:S(2)}) async-start(bf16[2,64,64,512]{3,2,0,1:T(8,128)(2,1)} %select_bitcast_fusion.2), calls=%async_computation | async-start | bytes 16777216 | tf_op jit(solution)/shard_map/all_to_all | solution.py:106
  268.2 413.0 %all-gather.10.cloned.1.call-start = ((), (), s32[]{:S(2)}) async-start(), calls=%async_computation.5 | async-start | bytes 8519680 | tf_op jit(solution)/shard_map/all_gather | solution.py:15
  478.1 240.1 %all-to-all-start.2 = ((bf16[2,64,64,512]{3,2,0,1:T(8,128)(2,1)}), bf16[2,64,64,512]{3,2,0,1:T(8,128)(2,1)}, u32[]{:S(2)}, u32[]{:S(2)}) async-start(bf16[2,64,64,512]{3,2,0,1:T(8,128)(2,1)} %select_bitcast_fusion), calls=%async_computation.2 | async-start | bytes 16777216 | tf_op jit(solution)/shard_map/all_to_all | solution.py:106
  496.2 432.5 %all-gather.6.cloned.1.call-start = ((), (), s32[]{:S(2)}) async-start(), calls=%async_computation.3 | async-start | bytes 7864320 | tf_op jit(solution)/shard_map/all_gather | solution.py:139
  496.2 171.6 %collective-permute-start = (bf16[2,64,512]{2,1,0:T(8,128)(2,1)S(1)}, bf16[2,64,512]{2,1,0:T(8,128)(2,1)S(1)}, u32[]{:S(2)}, u32[]{:S(2)}) collective-permute-start(bf16[2,64,512]{2,1,0:T(8,128)(2,1)S(1)} %get-tuple-element.256), channel_id=1, source_target_pairs={{0,4},{4,8},{8,12},{12,16},{16,20},{20,24},{24,28},{28,32},{32,36}... | collective-permute-start | bytes 393224 | tf_op jit(solution)/shard_map/ppermute | solution.py:23
  499.1 174.8 %collective-permute-start.1 = (bf16[2,64,512]{2,1,0:T(8,128)(2,1)S(1)}, bf16[2,64,512]{2,1,0:T(8,128)(2,1)}, u32[]{:S(2)}, u32[]{:S(2)}) collective-permute-start(bf16[2,64,512]{2,1,0:T(8,128)(2,1)S(1)} %get-tuple-element.257), channel_id=1, source_target_pairs={{4,0},{8,4},{12,8},{16,12},{20,16},{24,20},{28,24},{32,28},{36,32}... | collective-permute-start | bytes 393224 | tf_op jit(solution)/shard_map/ppermute | solution.py:26
  707.4 5.8 copy-start.13
  713.3 2.8 copy-start.7
  713.3 2.8 copy-start.15
  731.7 2.8 copy-start.6
  760.9 2.0 copy-start.3
  762.8 1.6 copy-start
  763.4 3.0 copy-start.4
  766.3 4.8 copy-start.1
  771.1 3.4 copy-start.5
  799.3 2.0 copy-start.3
  801.3 1.6 copy-start
  801.8 3.0 copy-start.4
  804.8 4.8 copy-start.1
  809.6 3.4 copy-start.5
  837.7 2.0 copy-start.3
  839.6 1.6 copy-start
  840.2 3.0 copy-start.4
  843.2 4.8 copy-start.1
  847.9 3.4 copy-start.5
Sparse Core Ops, SparseCore 0:
  44.1 221.0 all-gather.7
  272.8 221.2 all-gather.9
  853.9 74.7 all-gather.5
